TPU v7x, 32 devices: a whole 2x2x4 slice. The times are simulated.
32 devices in a mesh: hid: 8 (over y, x, core), ep: 4 (over z).
Axes of the slice: x: 2, y: 2, z: 4, core: 2. Of those that a mesh axis runs over, the one named last changes fastest.
Arguments:
- tokens: bfloat16 [2048, 2048], P('ep', 'hid'), may hold values from -6 to 6
- expert_ids: int32 [2048, 6], P('ep'), may hold values from 0 to 15, all different within a row; in each aligned block of 512 rows (0 to 511, 512 to 1023, ...) at most 256 rows name the same one
- gate_weights: float32 [2048, 6], P('ep'), may hold values from 0.1 to 1
- w_gate_up: bfloat16 [4, 5632, 2, 2048], P('ep', 'hid'), may hold values from -0.125 to 0.125
- w_down: bfloat16 [4, 5632, 2048], P('ep', 'hid'), may hold values from -0.21875 to 0.21875
Outputs:
- mixed: bfloat16 [2048, 2048], P('ep', 'hid')
Inputs may be any that keep to these rules, and one draw needn't show every extreme that they name: `expert_ids`: the 6 ids of a row differ. Among the 512 rows of one index of ep (aligned blocks of rows), no expert is named by more than 256 rows.
All inputs are finite; a program needn't handle non-finite values.
Results may differ from a plain program's by a relative error of at most 0.0064.
Values may be sent and summed in bfloat16 or wider, within the bound.
A program may use at most 64 MiB of HBM per device.

v0:
```python
import jax
import jax.numpy as jnp
from jax import lax
from jax.sharding import PartitionSpec as P

EXP_DEV = 4


def slot_numbers(ids, count):
    flat = ids.reshape(-1)
    onehot = (flat[:, None] == jnp.arange(count, dtype=jnp.int32)[None, :]).astype(jnp.int32)
    before = jnp.cumsum(onehot, axis=0) - onehot
    return jnp.sum(before * onehot, axis=1).reshape(ids.shape)


def on_device(tokens, expert_ids, gate_weights, w_gate_up, w_down):
    groups = lax.axis_size("ep")
    hid_count = lax.axis_size("hid")
    shards = hid_count // EXP_DEV
    experts = EXP_DEV * groups
    tok_rows = tokens.shape[0]
    width_local = tokens.shape[1]
    topk = expert_ids.shape[1]
    capacity = tok_rows * topk * 4 // (3 * experts)
    rows_per = groups * capacity
    slot = slot_numbers(expert_ids, experts)
    token_index = jnp.broadcast_to(jnp.arange(tok_rows, dtype=jnp.int32)[:, None], expert_ids.shape)
    table = (
        jnp.full((experts, capacity), tok_rows, dtype=jnp.int32)
        .at[expert_ids, slot]
        .set(token_index)
    )
    padded = jnp.concatenate([tokens, jnp.zeros((1, width_local), tokens.dtype)], axis=0)
    placed = padded[table].reshape(groups, EXP_DEV, capacity, width_local)
    arrived = lax.all_to_all(placed, "ep", split_axis=0, concat_axis=2, tiled=True)[0]
    repeated = jnp.repeat(arrived, shards, axis=0)
    outgoing = jnp.transpose(repeated, (1, 0, 2)).reshape(rows_per, hid_count * width_local)
    full_rows = lax.all_to_all(outgoing, "hid", split_axis=1, concat_axis=1, tiled=True)
    gate_up = jnp.einsum("rd,fgd->gfr", full_rows, w_gate_up[0], preferred_element_type=jnp.float32)
    hidden = (jax.nn.silu(gate_up[0]) * gate_up[1]).astype(jnp.bfloat16)
    partial_value = jnp.einsum("fr,fd->rd", hidden, w_down[0], preferred_element_type=jnp.float32)
    rounded = partial_value.astype(jnp.bfloat16)
    homed = lax.all_to_all(
        rounded.reshape(1, groups, capacity, rounded.shape[1]),
        "ep",
        split_axis=1,
        concat_axis=0,
        tiled=True,
    )
    moved = lax.all_to_all(homed, "hid", split_axis=3, concat_axis=0, tiled=True)
    grouped = moved.reshape(EXP_DEV, shards, groups, capacity, width_local).astype(jnp.float32)
    summed = jnp.sum(grouped, axis=1).astype(jnp.bfloat16)
    back = jnp.transpose(summed, (1, 0, 2, 3))
    flat = back.reshape(experts * capacity, width_local)
    picked = flat[expert_ids * capacity + slot]
    mixed = jnp.sum(picked.astype(jnp.float32) * gate_weights[:, :, None], axis=1)
    return mixed.astype(jnp.bfloat16)


def solution(mesh):
    return jax.shard_map(
        on_device,
        mesh=mesh,
        in_specs=(
            P("ep", "hid"),
            P("ep", None),
            P("ep", None),
            P("ep", "hid", None, None),
            P("ep", "hid", None),
        ),
        out_specs=P("ep", "hid"),
        check_vma=False,
    )
```

profile of v0, /device:TPU:0, one launch (start us, length us, event | category | flops | bytes accessed | tf_op | source)
XLA Modules:
  0.0 363.1 jit_solution(8262749961850203869)
XLA Ops:
  0.0 1.0 copy.60
  1.0 0.2 eq.29
  1.2 0.2 eq.25
  1.4 4.6 %reduce-window.6 = s32[16,24,128]{2,1,0:T(8,128)S(1)} reduce-window(s32[16,24,128]{2,1,0:T(8,128)S(1)} %fusion.12, s32[]{:T(128)} %constant.5.clone.1), window={size=1x1x128 pad=0_0x0_0x127_0}, to_apply=%region_0.0 | reduce-window | flops 6242304 | bytes 393220 | tf_op jit(solution)/shard_map/reduce-window
  6.0 0.4 slice_reduce_fusion
  6.4 0.2 reduce-window.9
  6.8 0.2 reshape.83
  7.0 0.2 reshape.77
  7.8 0.1 copy.64
  8.0 0.2 reshape.104
  8.2 0.2 reshape.106
  8.3 11.8 %scatter_custom_fusion = s32[4096]{0:T(1024)S(1)} fusion(s32[3072]{0:T(1024)S(1)} %reshape.104, s32[3072]{0:T(1024)S(1)} %reshape.106, s32[]{:T(128)} %constant.10.clone.1), kind=kCustom, calls=%fused_computation.31 | custom fusion | bytes 16388
  20.2 1.0 concatenate.6
  21.2 16.9 %gather_fusion = bf16[4096,256]{1,0:T(8,128)(2,1)} fusion(bf16[513,256]{1,0:T(8,128)(2,1)S(1)} %concatenate.6, s32[4096]{0:T(1024)S(1)} %broadcast_clamp_fusion), kind=kCustom, calls=%fused_computation | custom fusion | bytes 4210688 | tf_op jit(solution)/shard_map/gather | solution.py:34
  38.1 54.5 %all_to_all.51 = bf16[4,4,256,256]{3,2,1,0:T(8,128)(2,1)S(1)} all-to-all(bf16[4,4,256,256]{3,2,1,0:T(8,128)(2,1)} %bitcast.59), channel_id=1, replica_groups=mesh['hid'=8,'ep'=4] {'ep'}, dimensions={0} | all-to-all | bytes 4194304 | tf_op jit(solution)/shard_map/all_to_all | solution.py:35
  92.8 0.3 broadcast_in_dim.29
  93.1 52.6 %all_to_all.52 = bf16[1024,8,256]{2,0,1:T(8,128)(2,1)S(1)} all-to-all(bf16[1024,8,256]{2,0,1:T(8,128)(2,1)S(1)} %bitcast.55), channel_id=1, replica_groups=mesh['hid'=8,'ep'=4] {'hid'}, dimensions={1} | all-to-all | bytes 8388608 | tf_op jit(solution)/shard_map/all_to_all | solution.py:38
  145.6 4.3 %copy.66 = bf16[1024,8,256]{2,1,0:T(8,128)(2,1)} copy(bf16[1024,8,256]{2,0,1:T(8,128)(2,1)S(1)} %all_to_all.52) | data formatting | bytes 8388608 | tf_op jit(solution)/shard_map/all_to_all | solution.py:38
  150.0 7.4 %reshape.116 = bf16[1024,2048,1]{1,0,2:T(8,128)(2,1)} reshape(bf16[1024,8,256]{2,1,0:T(8,128)(2,1)} %copy.66) | data formatting | bytes 8388608 | tf_op jit(solution)/shard_map/all_to_all | solution.py:38
  157.4 12.0 %fusion.4 = f32[2,704,1024]{2,1,0:T(8,128)S(1)} fusion(bf16[1024,2048,1]{1,0,2:T(8,128)(2,1)} %reshape.116, bf16[704,2,2048]{2,1,0:T(2,128)(2,1)} %bitcast.64), kind=kOutput, calls=%fused_computation.10 | convolution fusion | flops 5905580032 | bytes 15728640 | tf_op jit(solution)/shard_map/rd,fgd->gfr/dot_general | solution.py:39
  169.4 3.9 %convolution_convert_fusion = bf16[1024,2048]{1,0:T(8,128)(2,1)S(1)} fusion(bf16[1,704,2048]{2,1,0:T(8,128)(2,1)S(1)} %copy-done, f32[2,704,1024]{2,1,0:T(8,128)S(1)} %fusion.4), kind=kOutput, calls=%fused_computation.6 | convolution fusion | flops 2959212544 | bytes 12845056 | tf_op jit(solution)/shard_map/fr,fd->rd/dot_general | solution.py:41
  173.3 96.3 %all_to_all.53 = bf16[1,4,256,2048]{3,2,0,1:T(8,128)(2,1)} all-to-all(bf16[1,4,256,2048]{3,2,0,1:T(8,128)(2,1)S(1)} %bitcast.60), channel_id=1, replica_groups=mesh['hid'=8,'ep'=4] {'ep'}, dimensions={1} | all-to-all | bytes 8388608 | tf_op jit(solution)/shard_map/all_to_all | solution.py:43
  269.6 7.5 %copy.69 = bf16[4,1,256,2048]{2,0,1,3:T(4,128)(2,1)} copy(bf16[4,1,256,2048]{3,2,0,1:T(8,128)(2,1)} %bitcast.56) | data formatting | bytes 8388608 | tf_op jit(solution)/shard_map/all_to_all | solution.py:43
  277.1 4.9 %all-to-all-start.3 = ((bf16[4,1,256,2048]{2,0,1,3:T(4,128)(2,1)}), bf16[4,1,256,2048]{2,0,1,3:T(4,128)(2,1)}, u32[]{:S(2)}, u32[]{:S(2)}) async-start(bf16[4,1,256,2048]{2,0,1,3:T(4,128)(2,1)} %copy.69), calls=%async_computation.3 | async-start | bytes 8388608 | tf_op jit(solution)/shard_map/all_to_all | solution.py:50
  282.1 0.2 reshape.98
  282.3 0.1 copy.74
  282.5 48.4 %all-to-all-done.3 = bf16[4,1,256,2048]{2,0,1,3:T(4,128)(2,1)} async-done(((bf16[4,1,256,2048]{2,0,1,3:T(4,128)(2,1)}), bf16[4,1,256,2048]{2,0,1,3:T(4,128)(2,1)}, u32[]{:S(2)}, u32[]{:S(2)}) %all-to-all-start.3) | async-done | bytes 4194336 | tf_op jit(solution)/shard_map/all_to_all | solution.py:50
  330.9 6.9 %reduce_sum.31 = bf16[4,4,256,256]{2,1,3,0:T(4,128)(2,1)} reduce(bf16[4,2,4,256,256]{3,2,4,1,0:T(4,128)(2,1)} %bitcast.17, bf16[]{:T(256)} %constant.9.clone.1), dimensions={1}, to_apply=%region_4.5 | reduce | flops 1048576 | bytes 6291458 | tf_op jit(solution)/shard_map/reduce_sum | solution.py:52
  337.8 3.0 copy.71
  340.8 13.0 %gather_fusion.1 = bf16[3072,256]{1,0:T(8,128)(2,1)} fusion(bf16[4096,256]{1,0:T(8,128)(2,1)S(1)} %bitcast.54, s32[3072]{0:T(1024)S(1)} %broadcast_clamp_fusion.1), kind=kCustom, calls=%fused_computation.1 | custom fusion | bytes 3158016 | tf_op jit(solution)/shard_map/gather | solution.py:55
  353.8 4.1 %reshape.115 = f32[512,6,256]{2,1,0:T(8,128)} reshape(bf16[3072,256]{1,0:T(8,128)(2,1)} %gather_fusion.1) | data formatting | bytes 4718592 | tf_op jit(solution)/shard_map/convert_element_type | solution.py:56
  357.9 5.2 %multiply_reduce_fusion = bf16[512,256]{1,0:T(8,128)(2,1)} fusion(f32[512,6,256]{2,1,0:T(8,128)} %reshape.115, f32[512,6]{1,0:T(8,128)S(1)} %copy.74), kind=kLoop, calls=%fused_computation.5 | loop fusion | flops 1441792 | bytes 3420160 | tf_op jit(solution)/shard_map/reduce_sum | solution.py:56
  (31 shorter events, 1.1 us)
Async XLA Ops:
  0.0 169.4 %copy-start = (bf16[1,704,2048]{2,1,0:T(8,128)(2,1)S(1)}, bf16[1,704,2048]{2,1,0:T(8,128)(2,1)}, u32[]{:S(2)}) copy-start(bf16[1,704,2048]{2,1,0:T(8,128)(2,1)} %param.9) | copy-start | bytes 8650756
  0.0 7.6 %copy-start.5 = (s32[2]{0:T(128)S(1)}, s32[2]{0:T(128)}, u32[]{:S(2)}) copy-start(s32[2]{0:T(128)} %constant.30) | copy-start | bytes 28
  0.0 7.7 %copy-start.4 = (s32[2]{0:T(128)S(1)}, s32[2]{0:T(128)}, u32[]{:S(2)}) copy-start(s32[2]{0:T(128)} %constant.33) | copy-start | bytes 28
  0.0 7.4 %copy-start.2 = (s32[512,6]{0,1:T(8,128)S(1)}, s32[512,6]{0,1:T(8,128)}, u32[]{:S(2)}) copy-start(s32[512,6]{0,1:T(8,128)} %param.6) | copy-start | bytes 36868
  277.1 5.2 %copy-start.3 = (f32[512,6]{0,1:T(8,128)S(1)}, f32[512,6]{0,1:T(8,128)}, u32[]{:S(2)}) copy-start(f32[512,6]{0,1:T(8,128)} %param.7) | copy-start | bytes 36868
  277.1 53.8 %all-to-all-start.3 = ((bf16[4,1,256,2048]{2,0,1,3:T(4,128)(2,1)}), bf16[4,1,256,2048]{2,0,1,3:T(4,128)(2,1)}, u32[]{:S(2)}, u32[]{:S(2)}) async-start(bf16[4,1,256,2048]{2,0,1,3:T(4,128)(2,1)} %copy.69), calls=%async_computation.3 | async-start | bytes 8388608 | tf_op jit(solution)/shard_map/all_to_all | solution.py:50
  353.8 9.3 %copy-start.1 = (bf16[1,704,2048]{2,1,0:T(8,128)(2,1)S(1)}, bf16[1,704,2048]{2,1,0:T(8,128)(2,1)}, u32[]{:S(2)}) copy-start(bf16[1,704,2048]{2,1,0:T(8,128)(2,1)} %param.9) | copy-start | bytes 8650756
where the time goes:
time: 364 us; the launch traced here: 363 us
  blocking collectives  203 us (56%)
  local copies, waits for them, and re-layouts  72.8 us (20%)
  waiting for transfers between devices  48.4 us (13%)
  other arithmetic  17.4 us (5%)
  matrix products  15.9 us (4%)
  starting transfers between devices  4.9 us (1%)
    all_to_all x1, blocking collectives, on_device(): lax.all_to_all(rounded.reshape(1, groups, capacity, rounded.shape[1]), 'e...  96.3 us
    all_to_all x1, blocking collectives, on_device(): lax.all_to_all(placed, 'ep', split_axis=0, concat_axis=2, tiled=True)[0]  54.5 us
    all_to_all x1, blocking collectives, on_device(): lax.all_to_all(outgoing, 'hid', split_axis=1, concat_axis=1, tiled=True)  52.6 us
    all_to_all x1, waiting for transfers between devices, on_device(): lax.all_to_all(homed, 'hid', split_axis=3, concat_axis=0, tiled=True)  48.4 us
    gather x1, local copies, waits for them, and re-layouts, on_device(): placed = padded[table].reshape(groups, EXP_DEV, capacity, width_local)  16.9 us
    unnamed x18, local copies, waits for them, and re-layouts  13.3 us
    gather x1, local copies, waits for them, and re-layouts, on_device(): picked = flat[expert_ids * capacity + slot]  13 us
    dot_general x1, matrix products, on_device(): jnp.einsum('rd,fgd->gfr', full_rows, w_gate_up[0], preferred_element_type...  12 us
  transfers between devices with their start and end apart: 1, of which 1 were waited for; matrix products, arithmetic and copies ran while one was open for 0% of the time, Pallas kernels for 0%

commit v1 on v0

--- a/solution.py
+++ b/solution.py
@@ -4,6 +4,13 @@
 from jax.sharding import PartitionSpec as P
 
 EXP_DEV = 4
+
+
+def stacked_exchange(shard, mesh_axis, split, join):
+    count = lax.axis_size(mesh_axis)
+    blocks = jnp.stack(jnp.split(shard, count, axis=split), axis=0)
+    blocks = lax.all_to_all(blocks, mesh_axis, split_axis=0, concat_axis=0)
+    return jnp.concatenate(blocks, axis=join)
 
 
 def slot_numbers(ids, count):
@@ -35,7 +42,7 @@
     arrived = lax.all_to_all(placed, "ep", split_axis=0, concat_axis=2, tiled=True)[0]
     repeated = jnp.repeat(arrived, shards, axis=0)
     outgoing = jnp.transpose(repeated, (1, 0, 2)).reshape(rows_per, hid_count * width_local)
-    full_rows = lax.all_to_all(outgoing, "hid", split_axis=1, concat_axis=1, tiled=True)
+    full_rows = stacked_exchange(outgoing, "hid", 1, 1)
     gate_up = jnp.einsum("rd,fgd->gfr", full_rows, w_gate_up[0], preferred_element_type=jnp.float32)
     hidden = (jax.nn.silu(gate_up[0]) * gate_up[1]).astype(jnp.bfloat16)
     partial_value = jnp.einsum("fr,fd->rd", hidden, w_down[0], preferred_element_type=jnp.float32)

time: 364 us -> 385 us (1.058)
  local copies, waits for them, and re-layouts: 72.8 us -> 91.7 us
    reshape x0 -> x3, local copies, waits for them, and re-layouts: none -> 18.9 us  [the longest x2 11.7 us: stacked_exchange(): return jnp.concatenate(blocks, axis=join)]
    all_to_all x2 -> x0, local copies, waits for them, and re-layouts: 11.7 us -> none  [on_device(): lax.all_to_all(outgoing, 'hid', split_axis=1, concat_axis=1, tiled=True)]
    unnamed x18, local copies, waits for them, and re-layouts: 13.3 us -> 17.4 us
where the time goes in v1:
time: 385 us; the launch traced here: 384 us
  blocking collectives  203 us (53%)
  local copies, waits for them, and re-layouts  91.7 us (24%)
  waiting for transfers between devices  48.4 us (13%)
  other arithmetic  19.4 us (5%)
  matrix products  15.9 us (4%)
  starting transfers between devices  4.9 us (1%)
    all_to_all x1, blocking collectives, on_device(): lax.all_to_all(rounded.reshape(1, groups, capacity, rounded.shape[1]), 'e...  96.3 us
    all_to_all x1, blocking collectives, on_device(): lax.all_to_all(placed, 'ep', split_axis=0, concat_axis=2, tiled=True)[0]  54.5 us
    all_to_all x1, blocking collectives, stacked_exchange(): blocks = lax.all_to_all(blocks, mesh_axis, split_axis=0, concat_axis=0)  52.6 us
    all_to_all x1, waiting for transfers between devices, on_device(): lax.all_to_all(homed, 'hid', split_axis=3, concat_axis=0, tiled=True)  48.4 us
    unnamed x18, local copies, waits for them, and re-layouts  17.4 us
    gather x1, local copies, waits for them, and re-layouts, on_device(): placed = padded[table].reshape(groups, EXP_DEV, capacity, width_local)  16.9 us
    gather x1, local copies, waits for them, and re-layouts, on_device(): picked = flat[expert_ids * capacity + slot]  14 us
    dot_general x1, matrix products, on_device(): jnp.einsum('rd,fgd->gfr', full_rows, w_gate_up[0], preferred_element_type...  12 us
  transfers between devices with their start and end apart: 1, of which 1 were waited for; matrix products, arithmetic and copies ran while one was open for 0% of the time, Pallas kernels for 0%

profile of v1, /device:TPU:0, one launch (start us, length us, event | category | flops | bytes accessed | tf_op | source)
XLA Modules:
  0.0 384.0 jit_solution(2429572062552008125)
XLA Ops:
  0.0 1.0 copy.70
  1.4 4.6 %reduce-window.6 = s32[16,24,128]{2,1,0:T(8,128)S(1)} reduce-window(s32[16,24,128]{2,1,0:T(8,128)S(1)} %fusion.20, s32[]{:T(128)} %constant.5.clone.1), window={size=1x1x128 pad=0_0x0_0x127_0}, to_apply=%region_0.0 | reduce-window | flops 6242304 | bytes 393220 | tf_op jit(solution)/shard_map/reduce-window
  6.0 0.4 slice_reduce_fusion
  6.4 0.2 reduce-window.9
  6.8 0.2 reshape.91
  7.0 0.2 reshape.82
  7.3 0.7 compare_select_fusion.1
  8.2 0.8 multiply_reduce_fusion.1
  9.0 0.8 and_reduce_fusion
  10.0 0.2 reshape.112
  10.3 11.8 %scatter_custom_fusion = s32[4096]{0:T(1024)S(1)} fusion(s32[3072]{0:T(1024)S(1)} %reshape.112, s32[3072]{0:T(1024)S(1)} %reshape.114, s32[]{:T(128)} %constant.10.clone.1), kind=kCustom, calls=%fused_computation.47 | custom fusion | bytes 16388
  22.2 1.0 concatenate.6
  23.2 16.9 %gather_fusion = bf16[4096,256]{1,0:T(8,128)(2,1)} fusion(bf16[513,256]{1,0:T(8,128)(2,1)S(1)} %concatenate.6, s32[4096]{0:T(1024)S(1)} %broadcast_clamp_fusion), kind=kCustom, calls=%fused_computation | custom fusion | bytes 4210688 | tf_op jit(solution)/shard_map/gather | solution.py:41
  40.1 54.5 %all_to_all.47 = bf16[4,4,256,256]{3,2,1,0:T(8,128)(2,1)S(1)} all-to-all(bf16[4,4,256,256]{3,2,1,0:T(8,128)(2,1)} %bitcast.103), channel_id=1, replica_groups=mesh['hid'=8,'ep'=4] {'ep'}, dimensions={0} | all-to-all | bytes 4194304 | tf_op jit(solution)/shard_map/all_to_all | solution.py:42
  94.8 1.6 copy.76
  96.4 3.9 %broadcast_in_dim.29 = bf16[4,2,1024,256]{3,1,0,2:T(2,128)(2,1)} broadcast(bf16[4,1024,256]{2,0,1:T(4,128)(2,1)S(1)} %copy.76), dimensions={0,2,3} | broadcast | bytes 6291456 | tf_op jit(solution)/shard_map/broadcast_in_dim | solution.py:43
  100.3 7.2 %reshape.84 = bf16[8,1024,256]{2,0,1:T(8,128)(2,1)} reshape(bf16[4,2,1024,256]{3,1,0,2:T(2,128)(2,1)} %broadcast_in_dim.29) | data formatting | bytes 8388608 | tf_op jit(solution)/shard_map/reshape | solution.py:43
  107.5 3.7 copy.91
  111.8 52.6 %all_to_all.48 = bf16[8,1024,256]{2,1,0:T(8,128)(2,1)S(1)} all-to-all(bf16[8,1024,256]{2,1,0:T(8,128)(2,1)S(1)} %fusion.9), channel_id=1, replica_groups=mesh['hid'=8,'ep'=4] {'hid'}, dimensions={0} | all-to-all | bytes 8388608 | tf_op jit(solution)/shard_map/all_to_all | solution.py:12
  164.4 4.3 %copy.77 = bf16[1024,8,256]{2,1,0:T(8,128)(2,1)} copy(bf16[1024,8,256]{2,0,1:T(8,128)(2,1)S(1)} %bitcast.99) | data formatting | bytes 8388608 | tf_op jit(solution)/shard_map/reshape | solution.py:13
  168.7 7.4 %reshape.124 = bf16[1024,2048,1]{1,0,2:T(8,128)(2,1)} reshape(bf16[1024,8,256]{2,1,0:T(8,128)(2,1)} %copy.77) | data formatting | bytes 8388608 | tf_op jit(solution)/shard_map/reshape | solution.py:13
  176.1 12.0 %fusion.4 = f32[2,704,1024]{2,1,0:T(8,128)S(1)} fusion(bf16[1024,2048,1]{1,0,2:T(8,128)(2,1)} %reshape.124, bf16[704,2,2048]{2,1,0:T(2,128)(2,1)} %bitcast.108), kind=kOutput, calls=%fused_computation.10 | convolution fusion | flops 5905580032 | bytes 15728640 | tf_op jit(solution)/shard_map/rd,fgd->gfr/dot_general | solution.py:46
  188.2 3.9 %convolution_convert_fusion = bf16[1024,2048]{1,0:T(8,128)(2,1)S(1)} fusion(bf16[1,704,2048]{2,1,0:T(8,128)(2,1)S(1)} %copy-done, f32[2,704,1024]{2,1,0:T(8,128)S(1)} %fusion.4), kind=kOutput, calls=%fused_computation.6 | convolution fusion | flops 2959212544 | bytes 12845056 | tf_op jit(solution)/shard_map/fr,fd->rd/dot_general | solution.py:48
  192.1 96.3 %all_to_all.49 = bf16[1,4,256,2048]{3,2,0,1:T(8,128)(2,1)} all-to-all(bf16[1,4,256,2048]{3,2,0,1:T(8,128)(2,1)S(1)} %bitcast.104), channel_id=1, replica_groups=mesh['hid'=8,'ep'=4] {'ep'}, dimensions={1} | all-to-all | bytes 8388608 | tf_op jit(solution)/shard_map/all_to_all | solution.py:50
  288.4 7.5 %copy.80 = bf16[4,1,256,2048]{2,0,1,3:T(4,128)(2,1)} copy(bf16[4,1,256,2048]{3,2,0,1:T(8,128)(2,1)} %bitcast.100) | data formatting | bytes 8388608 | tf_op jit(solution)/shard_map/all_to_all | solution.py:50
  295.8 4.9 %all-to-all-start.3 = ((bf16[4,1,256,2048]{2,0,1,3:T(4,128)(2,1)}), bf16[4,1,256,2048]{2,0,1,3:T(4,128)(2,1)}, u32[]{:S(2)}, u32[]{:S(2)}) async-start(bf16[4,1,256,2048]{2,0,1,3:T(4,128)(2,1)} %copy.80), calls=%async_computation.3 | async-start | bytes 8388608 | tf_op jit(solution)/shard_map/all_to_all | solution.py:57
  301.2 48.4 %all-to-all-done.3 = bf16[4,1,256,2048]{2,0,1,3:T(4,128)(2,1)} async-done(((bf16[4,1,256,2048]{2,0,1,3:T(4,128)(2,1)}), bf16[4,1,256,2048]{2,0,1,3:T(4,128)(2,1)}, u32[]{:S(2)}, u32[]{:S(2)}) %all-to-all-start.3) | async-done | bytes 4194336 | tf_op jit(solution)/shard_map/all_to_all | solution.py:57
  349.6 6.9 %reduce_sum.31 = bf16[4,4,256,256]{2,1,3,0:T(4,128)(2,1)} reduce(bf16[4,2,4,256,256]{3,2,4,1,0:T(4,128)(2,1)} %bitcast.25, bf16[]{:T(256)} %constant.9.clone.1), dimensions={1}, to_apply=%region_4.5 | reduce | flops 1048576 | bytes 6291458 | tf_op jit(solution)/shard_map/reduce_sum | solution.py:59
  356.5 4.3 %copy.82 = bf16[4,4,256,256]{3,2,1,0:T(8,128)(2,1)} copy(bf16[4,4,256,256]{2,0,3,1:T(4,128)(2,1)} %bitcast.101) | data formatting | bytes 4194304 | tf_op jit(solution)/shard_map/transpose | solution.py:60
  360.8 14.0 %gather_fusion.1 = bf16[3072,256]{1,0:T(8,128)(2,1)} fusion(bf16[4096,256]{1,0:T(8,128)(2,1)} %bitcast.89, s32[3072]{0:T(1024)S(1)} %broadcast_clamp_fusion.1), kind=kCustom, calls=%fused_computation.1 | custom fusion | bytes 3158016 | tf_op jit(solution)/shard_map/gather | solution.py:62
  374.8 4.0 %reshape.123 = f32[512,6,256]{2,1,0:T(8,128)} reshape(bf16[3072,256]{1,0:T(8,128)(2,1)} %gather_fusion.1) | data formatting | bytes 4718592 | tf_op jit(solution)/shard_map/convert_element_type | solution.py:63
  378.8 5.2 %multiply_reduce_fusion = bf16[512,256]{1,0:T(8,128)(2,1)} fusion(f32[512,6,256]{2,1,0:T(8,128)} %reshape.123, f32[512,6]{1,0:T(8,128)S(1)} %copy.85), kind=kLoop, calls=%fused_computation.5 | loop fusion | flops 1441792 | bytes 3420160 | tf_op jit(solution)/shard_map/reduce_sum | solution.py:63
  (34 shorter events, 2.3 us)
Async XLA Ops:
  0.0 188.2 %copy-start = (bf16[1,704,2048]{2,1,0:T(8,128)(2,1)S(1)}, bf16[1,704,2048]{2,1,0:T(8,128)(2,1)}, u32[]{:S(2)}) copy-start(bf16[1,704,2048]{2,1,0:T(8,128)(2,1)} %param.9) | copy-start | bytes 8650756
  295.8 5.2 %copy-start.1 = (f32[512,6]{0,1:T(8,128)S(1)}, f32[512,6]{0,1:T(8,128)}, u32[]{:S(2)}) copy-start(f32[512,6]{0,1:T(8,128)} %param.7) | copy-start | bytes 36868
  295.8 53.8 %all-to-all-start.3 = ((bf16[4,1,256,2048]{2,0,1,3:T(4,128)(2,1)}), bf16[4,1,256,2048]{2,0,1,3:T(4,128)(2,1)}, u32[]{:S(2)}, u32[]{:S(2)}) async-start(bf16[4,1,256,2048]{2,0,1,3:T(4,128)(2,1)} %copy.80), calls=%async_computation.3 | async-start | bytes 8388608 | tf_op jit(solution)/shard_map/all_to_all | solution.py:57
